TPU v7x, 256 devices: a whole 4x4x8 slice. The times are simulated.
256 devices in a mesh: band: 4 (over x), dom: 64 (over z, y, core).
Axes of the slice: x: 4, y: 4, z: 8, core: 2. Of those that a mesh axis runs over, the one named last changes fastest.
Arguments:
- orbitals: bfloat16 [256, 512, 2048], P('dom', None, 'band'), may hold values from -6 to 6
- projector_blocks: bfloat16 [4, 64, 96, 256, 128], P('band', 'dom'), may hold values from -0.1875 to 0.1875
- block_rows: int32 [4, 64, 96], P('band', 'dom'), may hold values from 0 to 15, as said below
- block_cols: int32 [4, 64, 96], P('band', 'dom'), may hold values from 0 to 26
- block_counts: int32 [4, 64], P('band', 'dom'), may hold values from 16 to 96, as said below
- strengths: float32 [73728], P('dom'), may hold values from -1.5 to 1.5
Outputs:
- applied: bfloat16 [256, 512, 2048], P('dom', None, 'band')
Inputs may be any that keep to these rules, and one draw needn't show every extreme that they name: `block_rows`: the slots of one device name distinct pairs of row block and column block. `block_counts`: some device has all 96 slots live.
All inputs are finite; a program needn't handle non-finite values.
Results may differ from a plain program's by a relative error of at most 0.0049.
Values may be sent and summed in bfloat16 or wider, within the bound.
A program may use at most 128 MiB of HBM per device.

v0:
```python
import jax
import jax.numpy as jnp
from jax import lax
from jax.sharding import PartitionSpec as P


def passed_along(value, axis, steps):
    count = lax.axis_size(axis)
    pairs = [(source, (source + steps) % count) for source in range(count)]
    return lax.ppermute(value, axis, pairs)


def padded(shard, sides, width):
    for axis, dim in sides:
        size, length = (lax.axis_size(axis), shard.shape[dim])
        up = [(i, (i + 1) % size) for i in range(size)]
        down = [(j, i) for i, j in up]
        last = lax.slice_in_dim(shard, length - width, length, axis=dim)
        leading = lax.slice_in_dim(shard, 0, width, axis=dim)
        before = lax.ppermute(last, axis, up)
        after = lax.ppermute(leading, axis, down)
        shard = jnp.concatenate([before, shard, after], axis=dim)
    return shard


def per_device(orbitals, projector_blocks, block_rows, block_cols, block_counts, strengths):
    slab_states = lax.all_to_all(orbitals, "dom", split_axis=1, concat_axis=0, tiled=True)
    state_total = slab_states.shape[0]
    planes = slab_states.shape[1]
    points = slab_states.shape[2]
    weights = projector_blocks[0, 0]
    slot_total = weights.shape[0]
    row_width = weights.shape[1]
    col_width = weights.shape[2]
    row_blocks = planes * points // row_width
    col_blocks = strengths.shape[0] // col_width
    slot_rows = block_rows[0, 0]
    slot_cols = block_cols[0, 0]
    live_total = block_counts[0, 0]
    live_weight = (jnp.arange(slot_total, dtype=jnp.int32) < live_total).astype(jnp.float32)
    picked = jnp.take(slab_states.reshape(state_total, row_blocks, row_width), slot_rows, axis=1)
    projected = jnp.einsum("skr,krc->kcs", picked, weights, preferred_element_type=jnp.float32)
    projected = projected * live_weight[:, None, None]
    partial_value = (
        jnp.zeros((3 * col_blocks, col_width, state_total), jnp.float32)
        .at[slot_cols]
        .add(projected)
    )
    partial_value = partial_value.reshape(3, col_blocks, col_width, state_total)
    scaling = strengths.reshape(col_blocks, col_width, 1)
    summed = lax.psum(partial_value, "band")
    below_part = passed_along(summed[2], "dom", 1)
    above_part = passed_along(summed[0], "dom", -1)
    scaled = (scaling * (summed[1] + below_part + above_part)).astype(jnp.bfloat16)
    neighbours = padded(scaled[None], (("dom", 0),), 1)
    neighbours = neighbours.reshape(3 * col_blocks, col_width, state_total)
    selected = jnp.take(neighbours, slot_cols, axis=0)
    returned = jnp.einsum("krc,kcs->skr", weights, selected, preferred_element_type=jnp.float32)
    returned = returned * live_weight[None, :, None]
    placed = (
        jnp.zeros((state_total, row_blocks, row_width), jnp.float32)
        .at[:, slot_rows, :]
        .add(returned)
    )
    result = placed.astype(jnp.bfloat16).reshape(state_total, planes, points)
    return lax.all_to_all(result, "dom", split_axis=0, concat_axis=1, tiled=True)


def solution(mesh):
    return jax.shard_map(
        per_device,
        mesh=mesh,
        in_specs=(
            P("dom", None, "band"),
            P("band", "dom", None, None, None),
            P("band", "dom", None),
            P("band", "dom", None),
            P("band", "dom"),
            P("dom"),
        ),
        out_specs=P("dom", None, "band"),
        check_vma=False,
    )
```

profile of v0, /device:TPU:8, one launch (start us, length us, event | category | flops | bytes accessed | tf_op | source)
XLA Modules:
  0.0 411.5 jit_solution(6211134194385298743)
XLA Ops:
  6.5 0.0 copy-start.4
  6.5 0.0 copy-start.5
  6.5 4.6 %copy.21 = bf16[4,512,512]{2,0,1:T(4,128)(2,1)} copy(bf16[4,512,512]{2,1,0:T(8,128)(2,1)} %param.6) | data formatting | bytes 4194304 | tf_op args[0]
  11.1 12.1 %all-to-all-start = ((bf16[4,512,512]{2,0,1:T(4,128)(2,1)}), bf16[4,512,512]{2,0,1:T(4,128)(2,1)S(1)}, u32[]{:S(2)}, u32[]{:S(2)}) async-start(bf16[4,512,512]{2,0,1:T(4,128)(2,1)} %copy.21), calls=%async_computation | async-start | bytes 4194304 | tf_op jit(solution)/shard_map/all_to_all | solution.py:27
  23.2 0.0 all-reduce.2.cloned.1.call-start
  23.9 0.0 copy-done.4
  23.9 0.0 copy-start.2
  23.9 0.0 copy-done.5
  24.0 0.5 copy-done.2
  24.5 50.0 %all-to-all-done = bf16[4,512,512]{2,0,1:T(4,128)(2,1)S(1)} async-done(((bf16[4,512,512]{2,0,1:T(4,128)(2,1)}), bf16[4,512,512]{2,0,1:T(4,128)(2,1)S(1)}, u32[]{:S(2)}, u32[]{:S(2)}) %all-to-all-start) | async-done | bytes 2097184 | tf_op jit(solution)/shard_map/all_to_all | solution.py:27
  74.5 1.9 copy.33
  76.4 4.1 reshape.93
  80.5 2.3 copy.23
  82.8 6.8 %gather_fusion = bf16[96,256,256]{2,1,0:T(8,128)(2,1)} fusion(bf16[256,16,256]{2,0,1:T(8,128)(2,1)S(1)} %copy.23, s32[1024]{0:T(1024)S(1)} %pad_clamp_fusion.1), kind=kCustom, calls=%fused_computation | custom fusion | bytes 25166208 | tf_op jit(solution)/shard_map/jit(_take)/gather | solution.py:41
  89.5 14.4 %multiply_bitcast_fusion = f32[96,128,256]{1,2,0:T(8,128)} fusion(f32[96]{0:T(128)S(1)} %get-tuple-element.7, bf16[1,1,96,256,128]{4,3,2,1,0:T(8,128)(2,1)} %param.7, bf16[96,256,256]{2,1,0:T(8,128)(2,1)} %gather_fusion, pred[96]{0:T(512)(128)(4,1)S(1)} %get-tuple-element.8), kind=kOutput, calls=%fused_computation.8 | convolution fusion | flops 1620049920 | bytes 31457760 | tf_op jit(solution)/shard_map/skr,krc->kcs/dot_general | solution.py:42
  103.9 12.6 %copy.24 = f32[96,128,256]{2,1,0:T(8,128)} copy(f32[96,128,256]{1,2,0:T(8,128)} %multiply_bitcast_fusion) | data formatting | bytes 25165824 | tf_op jit(solution)/shard_map/mul | solution.py:43
  116.5 0.4 broadcast_in_dim.35
  116.9 18.4 %scatter_fusion = f32[27,128,256]{2,1,0:T(8,128)S(1)} fusion(f32[27,128,256]{2,1,0:T(8,128)S(1)} %broadcast_in_dim.35, s32[96]{0:T(128)S(1)} %fusion.23, f32[96,128,256]{2,1,0:T(8,128)} %copy.24), kind=kCustom, calls=%fused_computation.2 | custom fusion | flops 3145728 | bytes 37749120 | tf_op jit(solution)/shard_map/scatter-add | solution.py:47
  135.3 0.0 copy-start
  135.3 0.0 copy-start.1
  135.4 1.8 copy-done
  137.1 0.0 all-reduce.2.cloned.1.call-update
  137.2 0.0 copy-start.6
  137.2 83.6 %all-reduce.2.cloned.1.call-done = f32[3,9,128,256]{3,2,1,0:T(8,128)} async-done(((f32[3,9,128,256]{3,2,1,0:T(8,128)}), f32[3,9,128,256]{3,2,1,0:T(8,128)}) %all-reduce.2.cloned.1.call-update) | async-done | bytes 3538960 | tf_op jit(solution)/shard_map/psum | solution.py:51
  220.8 1.8 slice_bitcast_fusion.1
  222.6 0.3 collective-permute-start
  222.9 1.7 collective-permute-start.1
  224.6 13.9 %collective-permute-done = f32[9,128,256]{2,1,0:T(8,128)S(1)} collective-permute-done((f32[9,128,256]{2,1,0:T(8,128)S(1)}, f32[9,128,256]{2,1,0:T(8,128)S(1)}, u32[]{:S(2)}, u32[]{:S(2)}) %collective-permute-start) | collective-permute-done | bytes 1179680 | tf_op jit(solution)/shard_map/ppermute | solution.py:10
  238.5 0.0 collective-permute-done.1
  238.5 0.0 copy-done.1
  238.5 1.6 fusion.21
  240.1 1.7 collective-permute-start.2
  241.8 0.5 collective-permute-start.3
  242.3 0.0 copy-done.6
  242.3 7.5 %collective-permute-done.2 = bf16[1,9,128,256]{3,2,1,0:T(8,128)(2,1)S(1)} collective-permute-done((bf16[1,9,128,256]{3,2,1,0:T(8,128)(2,1)S(1)}, bf16[1,9,128,256]{3,2,1,0:T(8,128)(2,1)S(1)}, u32[]{:S(2)}, u32[]{:S(2)}) %collective-permute-start.2) | collective-permute-done | bytes 589856 | tf_op jit(solution)/shard_map/ppermute | solution.py:20
  249.8 0.0 collective-permute-done.3
  249.8 0.2 pad_maximum_fusion
  250.0 6.1 %gather_fusion.1 = bf16[96,128,256]{2,1,0:T(8,128)(2,1)} fusion(bf16[27,128,256]{2,1,0:T(8,128)(2,1)S(1)} %bitcast.65, s32[1024]{0:T(1024)S(1)} %pad_clamp_fusion), kind=kCustom, calls=%fused_computation.1 | custom fusion | bytes 12583296 | tf_op jit(solution)/shard_map/jit(_take)/gather | solution.py:57
  256.0 14.3 %broadcast_multiply_fusion = f32[96,256,256]{2,1,0:T(8,128)} fusion(f32[96]{0:T(128)S(1)} %get-tuple-element.7, bf16[1,1,96,256,128]{4,3,2,1,0:T(8,128)(2,1)} %param.7, bf16[96,128,256]{2,1,0:T(8,128)(2,1)} %gather_fusion.1, pred[96]{0:T(512)(128)(4,1)S(1)} %compare_and_fusion.1), kind=kOutput, calls=%fused_computation.7 | convolution fusion | flops 1620049920 | bytes 37749216 | tf_op jit(solution)/shard_map/krc,kcs->skr/dot_general | solution.py:58
  270.3 0.0 copy-start.3
  270.3 2.4 broadcast_in_dim.33
  272.7 0.0 copy-done.3
  272.7 54.2 %scatter_fusion.1 = f32[256,16,256]{2,0,1:T(8,128)} fusion(f32[256,16,256]{2,0,1:T(8,128)} %broadcast_in_dim.33, s32[96]{0:T(128)S(1)} %copy-done.3, f32[96,256,256]{2,1,0:T(8,128)} %broadcast_multiply_fusion), kind=kCustom, calls=%fused_computation.3 | custom fusion | flops 6291456 | bytes 75497856 | tf_op jit(solution)/shard_map/scatter-add | solution.py:63
  327.0 2.4 convert_element_type.19
  329.4 2.4 copy.26
  331.8 3.4 copy.27
  335.2 68.0 %all_to_all.33 = bf16[256,8,512]{2,1,0:T(8,128)(2,1)S(1)} all-to-all(bf16[256,8,512]{2,1,0:T(8,128)(2,1)S(1)} %copy.27), channel_id=1, replica_groups=mesh['band'=4,'dom'=64] {'dom'}, dimensions={0} | all-to-all | bytes 4194304 | tf_op jit(solution)/shard_map/all_to_all | solution.py:66
  403.1 1.5 copy.32
  (6 shorter events, 0.0 us)
Async XLA Ops:
  6.5 17.4 %copy-start.4 = (s32[1,1,96]{2,1,0:T(1,128)S(1)}, s32[1,1,96]{2,1,0:T(1,128)}, u32[]{:S(2)}) copy-start(s32[1,1,96]{2,1,0:T(1,128)} %param.8) | copy-start | bytes 1156
  6.5 17.4 %copy-start.5 = (s32[1,1,96]{2,1,0:T(1,128)S(1)}, s32[1,1,96]{2,1,0:T(1,128)}, u32[]{:S(2)}) copy-start(s32[1,1,96]{2,1,0:T(1,128)} %param.9) | copy-start | bytes 1156
  11.1 63.4 %all-to-all-start = ((bf16[4,512,512]{2,0,1:T(4,128)(2,1)}), bf16[4,512,512]{2,0,1:T(4,128)(2,1)S(1)}, u32[]{:S(2)}, u32[]{:S(2)}) async-start(bf16[4,512,512]{2,0,1:T(4,128)(2,1)} %copy.21), calls=%async_computation | async-start | bytes 4194304 | tf_op jit(solution)/shard_map/all_to_all | solution.py:27
  23.2 197.6 %all-reduce.2.cloned.1.call-start = ((), (), s32[]{:S(2)}) async-start(), calls=%async_computation.2 | async-start | bytes 7077888 | tf_op jit(solution)/shard_map/psum | solution.py:51
  23.9 0.6 copy-start.2
  135.3 1.8 copy-start
  135.3 103.2 %copy-start.1 = (f32[1152]{0:T(1024)S(1)}, f32[1152]{0:T(1024)}, u32[]{:S(2)}) copy-start(f32[1152]{0:T(1024)} %param.11) | copy-start | bytes 13828
  137.2 105.1 %copy-start.6 = (s32[1,1,96]{2,1,0:T(1,128)S(1)}, s32[1,1,96]{2,1,0:T(1,128)}, u32[]{:S(2)}) copy-start(s32[1,1,96]{2,1,0:T(1,128)} %param.9) | copy-start | bytes 1156
  222.6 15.9 %collective-permute-start = (f32[9,128,256]{2,1,0:T(8,128)S(1)}, f32[9,128,256]{2,1,0:T(8,128)S(1)}, u32[]{:S(2)}, u32[]{:S(2)}) collective-permute-start(f32[9,128,256]{2,1,0:T(8,128)S(1)} %get-tuple-element.5), channel_id=1, source_target_pairs={{0,1},{1,2},{2,3},{3,4},{4,5},{5,6},{6,7},{7,8},{8,9},{9,10},{10,1... | collective-permute-start | bytes 3538952 | tf_op jit(solution)/shard_map/ppermute | solution.py:10
  222.9 15.6 %collective-permute-start.1 = (f32[9,128,256]{2,1,0:T(8,128)S(1)}, f32[9,128,256]{2,1,0:T(8,128)S(1)}, u32[]{:S(2)}, u32[]{:S(2)}) collective-permute-start(f32[9,128,256]{2,1,0:T(8,128)S(1)} %get-tuple-element.6), channel_id=1, source_target_pairs={{0,63},{1,0},{2,1},{3,2},{4,3},{5,4},{6,5},{7,6},{8,7},{9,8},{10,9... | collective-permute-start | bytes 3538952 | tf_op jit(solution)/shard_map/ppermute | solution.py:10
  240.1 9.7 %collective-permute-start.2 = (bf16[1,9,128,256]{3,2,1,0:T(8,128)(2,1)S(1)}, bf16[1,9,128,256]{3,2,1,0:T(8,128)(2,1)S(1)}, u32[]{:S(2)}, u32[]{:S(2)}) collective-permute-start(bf16[1,9,128,256]{3,2,1,0:T(8,128)(2,1)S(1)} %fusion.21), channel_id=1, source_target_pairs={{0,1},{1,2},{2,3},{3,4},{4,5},{5,6},{6,7},{7,8},{8,9},{9,10},{10,1... | collective-permute-start | bytes 1769480 | tf_op jit(solution)/shard_map/ppermute | solution.py:20
  241.8 8.0 %collective-permute-start.3 = (bf16[1,9,128,256]{3,2,1,0:T(8,128)(2,1)S(1)}, bf16[1,9,128,256]{3,2,1,0:T(8,128)(2,1)S(1)}, u32[]{:S(2)}, u32[]{:S(2)}) collective-permute-start(bf16[1,9,128,256]{3,2,1,0:T(8,128)(2,1)S(1)} %fusion.21), channel_id=1, source_target_pairs={{1,0},{2,1},{3,2},{4,3},{5,4},{6,5},{7,6},{8,7},{9,8},{10,9},{11,1... | collective-permute-start | bytes 1769480 | tf_op jit(solution)/shard_map/ppermute | solution.py:21
  270.3 2.4 copy-start.3
Sparse Core Ops, SparseCore 0:
  137.3 83.4 all-reduce.1
where the time goes:
time: 412 us
  waiting for transfers between devices  155 us (38%)
  other arithmetic  76.9 us (19%)
  blocking collectives  68 us (17%)
  local copies, waits for them, and re-layouts  52.5 us (13%)
  matrix products  28.7 us (7%)
  starting transfers between devices  16.3 us (4%)
  between operations  14.2 us (3%)
    psum x1, waiting for transfers between devices, per_device(): summed = lax.psum(partial_value, 'band')  83.6 us
    all_to_all x1, blocking collectives, per_device(): lax.all_to_all(result, 'dom', split_axis=0, concat_axis=1, tiled=True)  68 us
    scatter-add x1, other arithmetic, per_device(): placed = jnp.zeros((state_total, row_blocks, row_width), jnp.float32).at[...  54.2 us
    all_to_all x1, waiting for transfers between devices, per_device(): lax.all_to_all(orbitals, 'dom', split_axis=1, concat_axis=0, tiled=True)  50 us
    scatter-add x1, other arithmetic, per_device(): partial_value = jnp.zeros((3 * col_blocks, col_width, state_total), jnp.f...  18.4 us
    dot_general x1, matrix products, per_device(): jnp.einsum('skr,krc->kcs', picked, weights, preferred_element_type=jnp.fl...  14.4 us
    dot_general x1, matrix products, per_device(): jnp.einsum('krc,kcs->skr', weights, selected, preferred_element_type=jnp....  14.3 us
    ppermute x2, waiting for transfers between devices, passed_along(): return lax.ppermute(value, axis, pairs)  13.9 us
  transfers between devices with their start and end apart: 6, of which 4 were waited for; matrix products, arithmetic and copies ran while one was open for 0% of the time, Pallas kernels for 0%

commit v1 on v0

--- a/solution.py
+++ b/solution.py
@@ -48,7 +48,8 @@
     )
     partial_value = partial_value.reshape(3, col_blocks, col_width, state_total)
     scaling = strengths.reshape(col_blocks, col_width, 1)
-    summed = lax.psum(partial_value, "band")
+    shards = lax.all_gather(partial_value, "band", axis=0, tiled=False)
+    summed = shards.sum(axis=0)
     below_part = passed_along(summed[2], "dom", 1)
     above_part = passed_along(summed[0], "dom", -1)
     scaled = (scaling * (summed[1] + below_part + above_part)).astype(jnp.bfloat16)

time: 412 us -> 464 us (1.13)
  waiting for transfers between devices: 155 us -> 203 us
  other arithmetic: 76.9 us -> 82.4 us
    all_gather x0 -> x1, waiting for transfers between devices: none -> 131 us  [per_device(): shards = lax.all_gather(partial_value, 'band', axis=0, tiled=False)]
    psum x1 -> x0, waiting for transfers between devices: 83.6 us -> none  [per_device(): summed = lax.psum(partial_value, 'band')]
    reduce_sum x0 -> x1, other arithmetic: none -> 6.71 us  [per_device(): summed = shards.sum(axis=0)]
where the time goes in v1:
time: 464 us; the launch traced here: 463 us
  waiting for transfers between devices  203 us (44%)
  other arithmetic  82.4 us (18%)
  blocking collectives  68.2 us (15%)
  local copies, waits for them, and re-layouts  50.3 us (11%)
  matrix products  28.7 us (6%)
  starting transfers between devices  16.3 us (4%)
  between operations  14.2 us (3%)
    all_gather x1, waiting for transfers between devices, per_device(): shards = lax.all_gather(partial_value, 'band', axis=0, tiled=False)  131 us
    all_to_all x1, blocking collectives, per_device(): lax.all_to_all(result, 'dom', split_axis=0, concat_axis=1, tiled=True)  68.2 us
    scatter-add x1, other arithmetic, per_device(): placed = jnp.zeros((state_total, row_blocks, row_width), jnp.float32).at[...  54.3 us
    all_to_all x1, waiting for transfers between devices, per_device(): lax.all_to_all(orbitals, 'dom', split_axis=1, concat_axis=0, tiled=True)  50.3 us
    scatter-add x1, other arithmetic, per_device(): partial_value = jnp.zeros((3 * col_blocks, col_width, state_total), jnp.f...  18.4 us
    dot_general x1, matrix products, per_device(): jnp.einsum('skr,krc->kcs', picked, weights, preferred_element_type=jnp.fl...  14.4 us
    dot_general x1, matrix products, per_device(): jnp.einsum('krc,kcs->skr', weights, selected, preferred_element_type=jnp....  14.3 us
    ppermute x2, waiting for transfers between devices, passed_along(): return lax.ppermute(value, axis, pairs)  13.9 us
  transfers between devices with their start and end apart: 6, of which 4 were waited for; matrix products, arithmetic and copies ran while one was open for 0% of the time, Pallas kernels for 0%

profile of v1, /device:TPU:8, one launch (start us, length us, event | category | flops | bytes accessed | tf_op | source)
XLA Modules:
  0.0 462.6 jit_solution(10376801089242439904)
XLA Ops:
  6.5 0.0 copy-start.2
  6.5 0.0 copy-start.3
  6.5 4.6 copy.21
  11.1 12.1 %all-to-all-start = ((bf16[4,512,512]{2,0,1:T(4,128)(2,1)}), bf16[4,512,512]{2,0,1:T(4,128)(2,1)S(1)}, u32[]{:S(2)}, u32[]{:S(2)}) async-start(bf16[4,512,512]{2,0,1:T(4,128)(2,1)} %copy.21), calls=%async_computation | async-start | bytes 4194304 | tf_op jit(solution)/shard_map/all_to_all | solution.py:27
  23.2 0.2 all-gather.2.cloned.1.call-start
  24.1 0.0 copy-done.2
  24.1 0.0 copy-done.3
  24.2 50.3 %all-to-all-done = bf16[4,512,512]{2,0,1:T(4,128)(2,1)S(1)} async-done(((bf16[4,512,512]{2,0,1:T(4,128)(2,1)}), bf16[4,512,512]{2,0,1:T(4,128)(2,1)S(1)}, u32[]{:S(2)}, u32[]{:S(2)}) %all-to-all-start) | async-done | bytes 2097184 | tf_op jit(solution)/shard_map/all_to_all | solution.py:27
  74.5 1.9 copy.33
  76.4 4.1 reshape.90
  80.5 2.3 copy.23
  82.8 6.8 %gather_fusion = bf16[96,256,256]{2,1,0:T(8,128)(2,1)} fusion(bf16[256,16,256]{2,0,1:T(8,128)(2,1)S(1)} %copy.23, s32[1024]{0:T(1024)S(1)} %pad_clamp_fusion.1), kind=kCustom, calls=%fused_computation | custom fusion | bytes 25166208 | tf_op jit(solution)/shard_map/jit(_take)/gather | solution.py:41
  89.5 14.4 %multiply_bitcast_fusion = f32[96,128,256]{1,2,0:T(8,128)} fusion(f32[96]{0:T(128)S(1)} %get-tuple-element.7, bf16[1,1,96,256,128]{4,3,2,1,0:T(8,128)(2,1)} %param.7, bf16[96,256,256]{2,1,0:T(8,128)(2,1)} %gather_fusion, pred[96]{0:T(512)(128)(4,1)S(1)} %get-tuple-element.8), kind=kOutput, calls=%fused_computation.8 | convolution fusion | flops 1620049920 | bytes 31457760 | tf_op jit(solution)/shard_map/skr,krc->kcs/dot_general | solution.py:42
  103.9 12.6 %copy.24 = f32[96,128,256]{2,1,0:T(8,128)} copy(f32[96,128,256]{1,2,0:T(8,128)} %multiply_bitcast_fusion) | data formatting | bytes 25165824 | tf_op jit(solution)/shard_map/mul | solution.py:43
  116.5 0.4 broadcast_in_dim.35
  116.9 18.4 %scatter_fusion = f32[27,128,256]{2,1,0:T(8,128)S(1)} fusion(f32[27,128,256]{2,1,0:T(8,128)S(1)} %broadcast_in_dim.35, s32[96]{0:T(128)S(1)} %fusion.23, f32[96,128,256]{2,1,0:T(8,128)} %copy.24), kind=kCustom, calls=%fused_computation.2 | custom fusion | flops 3145728 | bytes 37749120 | tf_op jit(solution)/shard_map/scatter-add | solution.py:47
  135.4 0.0 copy-start
  135.4 1.7 copy-done
  137.1 0.0 all-gather.2.cloned.1.call-update
  137.1 130.9 %all-gather.2.cloned.1.call-done = f32[4,3,9,128,256]{4,3,2,1,0:T(8,128)} async-done(((f32[1,3,9,128,256]{4,3,2,1,0:T(8,128)}), f32[4,3,9,128,256]{4,3,2,1,0:T(8,128)}) %all-gather.2.cloned.1.call-update) | async-done | bytes 14155792 | tf_op jit(solution)/shard_map/all_gather | solution.py:51
  268.0 6.7 %reduce_sum.9 = f32[3,9,128,256]{3,2,1,0:T(8,128)S(1)} reduce(f32[4,3,9,128,256]{4,3,2,1,0:T(8,128)} %all-gather.2.cloned.1.call-done, f32[]{:T(128)} %constant.18.clone.1), dimensions={0}, to_apply=%region_1.2 | reduce | flops 2654208 | bytes 17694724 | tf_op jit(solution)/shard_map/reduce_sum | solution.py:52
  274.7 0.0 copy-start.1
  274.7 0.2 slice_bitcast_fusion.1
  274.9 0.1 collective-permute-start
  275.0 1.7 collective-permute-start.1
  276.8 13.9 %collective-permute-done = f32[9,128,256]{2,1,0:T(8,128)S(1)} collective-permute-done((f32[9,128,256]{2,1,0:T(8,128)S(1)}, f32[9,128,256]{2,1,0:T(8,128)S(1)}, u32[]{:S(2)}, u32[]{:S(2)}) %collective-permute-start) | collective-permute-done | bytes 1179680 | tf_op jit(solution)/shard_map/ppermute | solution.py:10
  290.6 0.0 collective-permute-done.1
  290.6 0.0 copy-done.1
  290.6 0.3 fusion.21
  291.0 1.7 collective-permute-start.2
  292.7 0.5 collective-permute-start.3
  293.2 7.5 %collective-permute-done.2 = bf16[1,9,128,256]{3,2,1,0:T(8,128)(2,1)S(1)} collective-permute-done((bf16[1,9,128,256]{3,2,1,0:T(8,128)(2,1)S(1)}, bf16[1,9,128,256]{3,2,1,0:T(8,128)(2,1)S(1)}, u32[]{:S(2)}, u32[]{:S(2)}) %collective-permute-start.2) | collective-permute-done | bytes 589856 | tf_op jit(solution)/shard_map/ppermute | solution.py:20
  300.7 0.0 collective-permute-done.3
  300.7 0.2 pad_maximum_fusion
  300.9 6.1 %gather_fusion.1 = bf16[96,128,256]{2,1,0:T(8,128)(2,1)} fusion(bf16[27,128,256]{2,1,0:T(8,128)(2,1)S(1)} %bitcast.65, s32[1024]{0:T(1024)S(1)} %pad_clamp_fusion), kind=kCustom, calls=%fused_computation.1 | custom fusion | bytes 12583296 | tf_op jit(solution)/shard_map/jit(_take)/gather | solution.py:58
  306.9 14.3 %broadcast_multiply_fusion = f32[96,256,256]{2,1,0:T(8,128)} fusion(f32[96]{0:T(128)S(1)} %get-tuple-element.7, bf16[1,1,96,256,128]{4,3,2,1,0:T(8,128)(2,1)} %param.7, bf16[96,128,256]{2,1,0:T(8,128)(2,1)} %gather_fusion.1, pred[96]{0:T(512)(128)(4,1)S(1)} %compare_and_fusion.1), kind=kOutput, calls=%fused_computation.7 | convolution fusion | flops 1620049920 | bytes 37749216 | tf_op jit(solution)/shard_map/krc,kcs->skr/dot_general | solution.py:59
  321.2 2.4 broadcast_in_dim.33
  323.7 54.3 %scatter_fusion.1 = f32[256,16,256]{2,0,1:T(8,128)} fusion(f32[256,16,256]{2,0,1:T(8,128)} %broadcast_in_dim.33, s32[96]{0:T(128)S(1)} %fusion.22, f32[96,256,256]{2,1,0:T(8,128)} %broadcast_multiply_fusion), kind=kCustom, calls=%fused_computation.3 | custom fusion | flops 6291456 | bytes 75497856 | tf_op jit(solution)/shard_map/scatter-add | solution.py:64
  377.9 2.4 convert_element_type.19
  380.4 2.4 copy.26
  382.7 3.4 copy.27
  386.1 68.2 %all_to_all.33 = bf16[256,8,512]{2,1,0:T(8,128)(2,1)S(1)} all-to-all(bf16[256,8,512]{2,1,0:T(8,128)(2,1)S(1)} %copy.27), channel_id=1, replica_groups=mesh['band'=4,'dom'=64] {'dom'}, dimensions={0} | all-to-all | bytes 4194304 | tf_op jit(solution)/shard_map/all_to_all | solution.py:67
  454.3 1.5 copy.32
  (6 shorter events, 0.0 us)
Async XLA Ops:
  6.5 17.5 %copy-start.2 = (s32[1,1,96]{2,1,0:T(1,128)S(1)}, s32[1,1,96]{2,1,0:T(1,128)}, u32[]{:S(2)}) copy-start(s32[1,1,96]{2,1,0:T(1,128)} %param.8) | copy-start | bytes 1156
  6.5 17.6 %copy-start.3 = (s32[1,1,96]{2,1,0:T(1,128)S(1)}, s32[1,1,96]{2,1,0:T(1,128)}, u32[]{:S(2)}) copy-start(s32[1,1,96]{2,1,0:T(1,128)} %param.9) | copy-start | bytes 1156
  11.1 63.4 %all-to-all-start = ((bf16[4,512,512]{2,0,1:T(4,128)(2,1)}), bf16[4,512,512]{2,0,1:T(4,128)(2,1)S(1)}, u32[]{:S(2)}, u32[]{:S(2)}) async-start(bf16[4,512,512]{2,0,1:T(4,128)(2,1)} %copy.21), calls=%async_computation | async-start | bytes 4194304 | tf_op jit(solution)/shard_map/all_to_all | solution.py:27
  23.2 244.8 %all-gather.2.cloned.1.call-start = ((), (), s32[]{:S(2)}) async-start(), calls=%async_computation.2 | async-start | bytes 17694720 | tf_op jit(solution)/shard_map/all_gather | solution.py:51
  135.4 1.7 copy-start
  274.7 15.9 %copy-start.1 = (f32[1152]{0:T(1024)S(1)}, f32[1152]{0:T(1024)}, u32[]{:S(2)}) copy-start(f32[1152]{0:T(1024)} %param.11) | copy-start | bytes 13828
  274.9 15.7 %collective-permute-start = (f32[9,128,256]{2,1,0:T(8,128)S(1)}, f32[9,128,256]{2,1,0:T(8,128)S(1)}, u32[]{:S(2)}, u32[]{:S(2)}) collective-permute-start(f32[9,128,256]{2,1,0:T(8,128)S(1)} %get-tuple-element.5), channel_id=1, source_target_pairs={{0,1},{1,2},{2,3},{3,4},{4,5},{5,6},{6,7},{7,8},{8,9},{9,10},{10,1... | collective-permute-start | bytes 3538952 | tf_op jit(solution)/shard_map/ppermute | solution.py:10
  275.0 15.6 %collective-permute-start.1 = (f32[9,128,256]{2,1,0:T(8,128)S(1)}, f32[9,128,256]{2,1,0:T(8,128)S(1)}, u32[]{:S(2)}, u32[]{:S(2)}) collective-permute-start(f32[9,128,256]{2,1,0:T(8,128)S(1)} %get-tuple-element.6), channel_id=1, source_target_pairs={{0,63},{1,0},{2,1},{3,2},{4,3},{5,4},{6,5},{7,6},{8,7},{9,8},{10,9... | collective-permute-start | bytes 3538952 | tf_op jit(solution)/shard_map/ppermute | solution.py:10
  291.0 9.7 %collective-permute-start.2 = (bf16[1,9,128,256]{3,2,1,0:T(8,128)(2,1)S(1)}, bf16[1,9,128,256]{3,2,1,0:T(8,128)(2,1)S(1)}, u32[]{:S(2)}, u32[]{:S(2)}) collective-permute-start(bf16[1,9,128,256]{3,2,1,0:T(8,128)(2,1)S(1)} %fusion.21), channel_id=1, source_target_pairs={{0,1},{1,2},{2,3},{3,4},{4,5},{5,6},{6,7},{7,8},{8,9},{9,10},{10,1... | collective-permute-start | bytes 1769480 | tf_op jit(solution)/shard_map/ppermute | solution.py:20
  292.7 8.0 %collective-permute-start.3 = (bf16[1,9,128,256]{3,2,1,0:T(8,128)(2,1)S(1)}, bf16[1,9,128,256]{3,2,1,0:T(8,128)(2,1)S(1)}, u32[]{:S(2)}, u32[]{:S(2)}) collective-permute-start(bf16[1,9,128,256]{3,2,1,0:T(8,128)(2,1)S(1)} %fusion.21), channel_id=1, source_target_pairs={{1,0},{2,1},{3,2},{4,3},{5,4},{6,5},{7,6},{8,7},{9,8},{10,9},{11,1... | collective-permute-start | bytes 1769480 | tf_op jit(solution)/shard_map/ppermute | solution.py:21
Sparse Core Ops, SparseCore 0:
  137.2 130.6 all-gather.1
